TPU v7x, 128 devices: a whole 4x4x4 slice. The times are simulated.
128 devices in a mesh: row: 4 (over y), col: 32 (over z, x, core).
Axes of the slice: x: 4, y: 4, z: 4, core: 2. Of those that a mesh axis runs over, the one named last changes fastest.
Arguments:
- lower_panel: float32 [32, 6, 5, 2, 256, 256], P('col', None, None, None, 'row'), may hold values from -0.0625 to 0.0625
- diag_inverse: float32 [32, 6, 2, 256, 256], P('col', None, None, 'row'), may hold values from -3 to 3, as said below
- structure: int32 [32, 6, 5], P('col'), may hold values 0 or 1
Outputs:
- sel_panel: float32 [32, 6, 5, 2, 256, 256], P('col', None, None, None, 'row')
- sel_diag: float32 [32, 6, 2, 256, 256], P('col', None, None, 'row')
Inputs may be any that keep to these rules, and one draw needn't show every extreme that they name: Every block diag_inverse[c, s, k] equals its own transpose.
All inputs are finite; a program needn't handle non-finite values. No bound on the sum of `structure` on one device may be relied on, other than what follows from the above.
Results may differ from a plain program's by a relative error of at most 0.0001.
Values sent between devices are 32-bit elements; how exact they have to be, the bound alone decides.
A program may use at most 128 MiB of HBM per device.

v0:
```python
import functools

import jax
import jax.numpy as jnp
from jax import lax
from jax.experimental import pallas as pl
from jax.experimental.pallas import tpu as pltpu
from jax.sharding import PartitionSpec as P

LEVELS = 6
MESH = pl.DeviceIdType.MESH
F32 = jnp.float32
BF16 = jnp.bfloat16
W = 256

X_AT = (None, 1, 3)
D_AT = (0, 2, 5)


def split(x):
    high = x.astype(BF16)
    return high, (x - high.astype(F32)).astype(BF16)


def mm(a, b):
    return jnp.dot(a, b, preferred_element_type=F32)


def kernel(
    lp, dg, panel, diag,
    f012, f3, f4, f5, gh, gl, xh, xl, rb1, rb2, rb3, rb4, lh, ll, pk, yo, zo, zb, dl,
    p1r, s0, s1, s2, s3, s4, ys, yr, xs, xr, cs, cr, os, ls,
):
    row = lax.axis_index("row")
    col = lax.axis_index("col")
    core = lax.rem(col, 2)
    xpos = lax.rem(col // 2, 4)
    plane = (col // 8) * 8
    up, down = lax.rem(row + 1, 4), lax.rem(row + 3, 4)
    xup, xdown = lax.rem(xpos + 1, 4), lax.rem(xpos + 3, 4)
    xfar = lax.rem(xpos + 2, 4)
    to_row = lambda r: {"row": r, "col": col}
    to_x = lambda x: {"row": row, "col": plane + 2 * x + core}
    other = {"row": row, "col": col + 1 - 2 * core}
    rbs = (None, rb1, rb2, rb3, rb4)
    my_rows = pl.ds(pl.multiple_of(row * 64, 64), 64)

    def remote(src, dst, send, recv, device):
        return pltpu.make_async_remote_copy(
            src_ref=src, dst_ref=dst, send_sem=send, recv_sem=recv, device_id=device, device_id_type=MESH
        )

    def pieces(d, j):
        kk = lax.rem(j, 2)
        if d <= 2:
            xx = lax.rem(j // 2, 4)
            part = pl.ds(pl.multiple_of(lax.rem(j, 8) * 8, 8), 8)
            out = [(dg.at[d, :, part], f012.at[D_AT[d], :, row, xx, kk])]
            if d:
                out.append((lp.at[d, 0:d, :, part], f012.at[X_AT[d] : X_AT[d] + d, :, row, xx, kk]))
            return out
        part = pl.ds(pl.multiple_of(kk * 32, 32), 32)
        buf = f3 if d == 3 else f4
        return [
            (dg.at[d, :, part], buf.at[d, :, row, kk]),
            (lp.at[d, 0:d, :, part], buf.at[0:d, :, row, kk]),
        ]

    sends = (s0, s1, s2, s3, s4)

    def home_copy(d, i, j):
        src, dst = pieces(d, j)[i]
        return remote(src, dst, sends[d].at[j - 1, i], p1r.at[d, i], {"row": row, "col": col + j})

    def is_home(d):
        return lax.rem(col, 2 ** (5 - d)) == 0

    def n_pieces(d):
        return 2 if d else 1

    def home_start(d):
        @pl.when(is_home(d))
        def _():
            for i, (src, dst) in enumerate(pieces(d, 0)):
                pltpu.make_async_copy(src, dst, p1r.at[d, i]).start()

            def step(j, carry):
                for i in range(n_pieces(d)):
                    home_copy(d, i, j).start()
                return carry

            lax.fori_loop(1, 2 ** (5 - d), step, 0)

    def home_finish(d):
        @pl.when(is_home(d))
        def _():
            def step(j, carry):
                for i in range(n_pieces(d)):
                    home_copy(d, i, j).wait_send()
                return carry

            lax.fori_loop(1, 2 ** (5 - d), step, 0)

    def piece_wait(d):
        for i, (_, dst) in enumerate(pieces(d, lax.rem(col, 8))):
            pltpu.make_async_copy(dst, dst, p1r.at[d, i]).wait()

    def y_slice(n, r, half=None):
        h = slice(None) if half is None else half
        if n == 0:
            return f012.at[:, h, r, xpos, core]
        if n == 1:
            return f3.at[:, h, r, core]
        if n == 2:
            return f4.at[:, h, r, core]
        return f5.at[n - 3, h, r]

    def y_copy(n, q):
        src = lp.at[5, n - 3] if n >= 3 else y_slice(n, row)
        if q == 0:
            args = (src, y_slice(n, row), up)
        elif q == 1:
            args = (src, y_slice(n, row), down)
        elif q == 2:
            args = (y_slice(n, down, 0), y_slice(n, down, 0), up)
        else:
            args = (y_slice(n, up, 1), y_slice(n, up, 1), down)
        return remote(args[0], args[1], ys.at[n, q], yr.at[n, q], to_row(args[2]))

    def y_first(n):
        y_copy(n, 0).start()
        y_copy(n, 1).start()

    def y_forward(n):
        y_copy(n, 0).wait_recv()
        y_copy(n, 2).start()
        y_copy(n, 1).wait_recv()
        y_copy(n, 3).start()

    def y_done(n):
        y_copy(n, 2).wait_recv()
        y_copy(n, 3).wait_recv()

    def x_copy(q):
        own = f012.at[:, :, :, xpos, core]
        if q == 0:
            args = (own, xup)
        elif q == 1:
            args = (own, xdown)
        elif q == 2:
            args = (f012.at[:, 0, :, xdown, core], xup)
        else:
            args = (f012.at[:, 1, :, xup, core], xdown)
        return remote(args[0], args[0], xs.at[q], xr.at[q], to_x(args[1]))

    def core_copy(q):
        if q < 4:
            ref = f012.at[:, :, :, (xpos, xdown, xup, xfar)[q], core]
        elif q == 4:
            ref = f3.at[:, :, :, core]
        else:
            ref = f4.at[:, :, :, core]
        return remote(ref, ref, cs.at[q], cr.at[q], other)

    leaf_own = pltpu.make_async_copy(lp.at[5], f5.at[:, :, row], ls.at[0])
    leaf_own.start()
    d_leaf = pltpu.make_async_copy(dg.at[5], dl.at[0], ls.at[1])
    d_leaf.start()
    d_root = pltpu.make_async_copy(dg.at[0], dl.at[1], ls.at[2])
    d_root.start()

    for d in range(5):
        home_start(d)
    y_first(3)
    y_first(4)
    for d in range(3):
        piece_wait(d)
    y_first(0)
    piece_wait(3)
    y_first(1)
    piece_wait(4)
    y_first(2)
    for n in range(5, 8):
        y_first(n)

    zb[...] = jnp.zeros_like(zb)
    zeros = [pltpu.make_async_copy(zb.at[0 : 5 - d], panel.at[d, d:5], os.at[0, d]) for d in range(5)]
    for copy in zeros:
        copy.start()

    y_forward(0)
    y_done(0)
    x_copy(0).start()
    x_copy(1).start()
    core_copy(0).start()
    y_forward(1)
    x_copy(0).wait_recv()
    x_copy(2).start()
    core_copy(1).start()
    x_copy(1).wait_recv()
    x_copy(3).start()
    core_copy(2).start()
    y_forward(2)
    y_done(1)
    core_copy(4).start()
    x_copy(2).wait_recv()
    x_copy(3).wait_recv()
    core_copy(3).start()
    y_forward(3)
    y_forward(4)

    d_root.wait()
    root_out = pltpu.make_async_copy(dl.at[1], diag.at[0], os.at[2, 0])
    root_out.start()
    for q in range(4):
        core_copy(q).wait_recv()

    def block(d, a, part):
        if d <= 2:
            return f012[X_AT[d] + a, part].reshape(W, W)
        if d == 3:
            return f3[a, part].reshape(W, W)
        if d == 4:
            return f4[a, part].reshape(W, W)
        return f5[a, part].reshape(W, W)

    def d_block(d, part):
        if d <= 2:
            return f012[D_AT[d], part].reshape(W, W)
        return (f3 if d == 3 else f4)[d, part].reshape(W, W)

    def put(high, low, rows, cols, real, imag):
        for m, value in enumerate((real, imag, real + imag)):
            h, l = split(value)
            high[m, rows, cols] = h
            low[m, rows, cols] = l

    def prepare(d):
        def step(f, carry):
            rows = pl.ds(pl.multiple_of(f * W, W), W)
            a = d - 1 - f
            put(xh, xl, rows, slice(None), block(d, a, 0), block(d, a, 1))
            return carry

        lax.fori_loop(0, d, step, 0)

    def three(high, low, rows, depth):
        out = []
        for m in range(3):
            a_high = high[m, rows, 0:depth]
            b_high = xh[m, 0:depth, :]
            acc = mm(a_high, b_high) + mm(a_high, xl[m, 0:depth, :])
            out.append(acc + mm(low[m, rows, 0:depth], b_high))
        return out[1] - out[0], out[0] + out[1] - out[2]

    put(gh, gl, slice(0, W), slice(0, W), d_block(0, 0), d_block(0, 1))

    outs = []

    def level(d):
        prepare(d)
        rb = rbs[d]
        depth = d * W
        new = slice(depth, depth + W)

        def step(e, carry):
            at = pl.ds(pl.multiple_of(e * W, W), W)
            real, imag = three(gh, gl, at, depth)
            last = (e == d).astype(F32)
            real = real + last * d_block(d, 0)
            imag = imag + last * d_block(d, 1)
            slot = jnp.where(e == d, d, d - 1 - e)
            rb[slot, 0] = real
            rb[slot, 1] = imag
            put(gh, gl, at, new, real, imag)
            put(gh, gl, new, at, real.T, imag.T)
            return carry

        lax.fori_loop(0, d + 1, step, 0)
        copies = [
            pltpu.make_async_copy(rb.at[0:d, :, my_rows], panel.at[d, 0:d], os.at[1, d]),
            pltpu.make_async_copy(rb.at[d, :, my_rows], diag.at[d], os.at[2, d]),
        ]
        for copy in copies:
            copy.start()
        outs.extend(copies)

    level(1)
    level(2)
    y_done(2)
    core_copy(5).start()
    core_copy(4).wait_recv()
    level(3)
    y_forward(5)
    y_forward(6)
    core_copy(5).wait_recv()
    level(4)
    y_forward(7)
    leaf_own.wait()
    for n in range(3, 8):
        y_done(n)

    prepare(5)

    def pick(x):
        out = x[:, 0:64]
        for r in range(1, 4):
            out = jnp.where(row == r, x[:, 64 * r : 64 * r + 64], out)
        return out

    def pack(f, carry):
        rows = pl.ds(pl.multiple_of(f * W, W), W)
        real, imag = pick(block(5, 4 - f, 0)), pick(block(5, 4 - f, 1))
        rh, rl = split(real)
        ih, il = split(imag)
        pk[rows, :] = jnp.concatenate([v.astype(F32) for v in (rh, ih, rl, il)], axis=1).astype(BF16)
        return carry

    lax.fori_loop(0, 5, pack, 0)

    def columns(e, carry):
        at = pl.ds(pl.multiple_of(e * W, W), W)
        p = pk[...]
        a = mm(gh[0, at, :], p) + mm(gl[0, at, :], p)
        b = mm(gh[1, at, :], p) + mm(gl[1, at, :], p)
        real = b[:, 64:128] + b[:, 192:256] - a[:, 0:64] - a[:, 128:192]
        imag = -(a[:, 64:128] + a[:, 192:256] + b[:, 0:64] + b[:, 128:192])
        flipped = jnp.concatenate([real, imag], axis=1).T
        put(lh, ll, slice(320, 384), at, flipped[0:64], flipped[64:128])
        mine = pl.ds(pl.multiple_of(e * W + row * 64, 64), 64)
        to = pl.ds(pl.multiple_of(e * 64, 64), 64)
        for m in range(3):
            lh[m, to, :] = gh[m, mine, :]
            ll[m, to, :] = gl[m, mine, :]
        return carry

    lax.fori_loop(0, 5, columns, 0)
    real, imag = three(lh, ll, slice(0, 384), 5 * W)
    for e in range(5):
        yo[4 - e, 0] = real[64 * e : 64 * e + 64]
        yo[4 - e, 1] = imag[64 * e : 64 * e + 64]
    d_leaf.wait()
    zo[0] = dl[0, 0] + real[320:384]
    zo[1] = dl[0, 1] + imag[320:384]
    copies = [
        pltpu.make_async_copy(yo, panel.at[5], os.at[1, 5]),
        pltpu.make_async_copy(zo, diag.at[5], os.at[2, 5]),
    ]
    for copy in copies:
        copy.start()

    for d in range(5):
        home_finish(d)
    for n in range(8):
        for q in range(4):
            y_copy(n, q).wait_send()
    for q in range(4):
        x_copy(q).wait_send()
    for q in range(6):
        core_copy(q).wait_send()
    for copy in zeros + [root_out] + outs + copies:
        copy.wait()


def inverse_blocks(lp, dg):
    dma = pltpu.SemaphoreType.DMA
    vmem = pltpu.VMEM
    side = 5 * W
    any_spec = pl.BlockSpec(memory_space=pl.ANY)
    return pl.pallas_call(
        kernel,
        out_shape=(
            jax.ShapeDtypeStruct((6, 5, 2, 64, W), F32),
            jax.ShapeDtypeStruct((6, 2, 64, W), F32),
        ),
        in_specs=[any_spec] * 2,
        out_specs=(any_spec, any_spec),
        scratch_shapes=[
            vmem((6, 2, 4, 4, 2, 8, W), F32),
            vmem((4, 2, 4, 2, 32, W), F32),
            vmem((5, 2, 4, 2, 32, W), F32),
            vmem((5, 2, 4, 64, W), F32),
            vmem((3, side, side), BF16),
            vmem((3, side, side), BF16),
            vmem((3, side, W), BF16),
            vmem((3, side, W), BF16),
            vmem((2, 2, W, W), F32),
            vmem((3, 2, W, W), F32),
            vmem((4, 2, W, W), F32),
            vmem((5, 2, W, W), F32),
            vmem((3, 384, side), BF16),
            vmem((3, 384, side), BF16),
            vmem((side, W), BF16),
            vmem((5, 2, 64, W), F32),
            vmem((2, 64, W), F32),
            vmem((5, 2, 64, W), F32),
            vmem((2, 2, 64, W), F32),
            dma((5, 2)),
            dma((31, 1)),
            dma((15, 2)),
            dma((7, 2)),
            dma((3, 2)),
            dma((1, 2)),
            dma((8, 4)),
            dma((8, 4)),
            dma((4,)),
            dma((4,)),
            dma((6,)),
            dma((6,)),
            dma((3, 6)),
            dma((3,)),
        ],
        compiler_params=pltpu.CompilerParams(vmem_limit_bytes=66_000_000, has_side_effects=True),
        name="inverse_blocks",
    )(lp, dg)


def body(lower_panel, diag_inverse, structure):
    masked = lower_panel[0] * structure[0].astype(F32)[:, :, None, None, None]
    panel, diag = inverse_blocks(masked, diag_inverse[0])
    position = lax.axis_index("col")
    strides = 2 ** (5 - jnp.arange(LEVELS))
    active = position % strides == 0
    panel = jnp.where(active[:, None, None, None, None], panel, 0.0)
    diag = jnp.where(active[:, None, None, None], diag, 0.0)
    return panel[None], diag[None]


def solution(mesh):
    in_specs = (
        P("col", None, None, None, "row", None),
        P("col", None, None, "row", None),
        P("col", None, None),
    )
    out_specs = (P("col", None, None, None, "row", None), P("col", None, None, "row", None))
    return jax.shard_map(body, mesh=mesh, in_specs=in_specs, out_specs=out_specs, check_vma=False)
```

profile of v0, /device:TPU:1, one launch (start us, length us, event | category | flops | bytes accessed | tf_op | source)
XLA Modules:
  0.0 113.6 jit_solution(18330577264535860610)
XLA Ops:
  0.6 0.1 fusion
  0.8 0.8 copy.5
  1.5 4.6 %bitcast_multiply_fusion.lp = f32[6,5,2,64,256]{4,3,2,1,0:T(8,128)} fusion(f32[1,6,5,2,64,256]{5,4,3,2,1,0:T(8,128)} %param.3, f32[6,5]{1,0:T(8,128)S(1)} %convert_bitcast_fusion), kind=kLoop, calls=%fused_computation | loop fusion | flops 983040 | bytes 7864440 | tf_op jit(solution)/shard_map/mul | solution.py:419
  6.1 101.7 %inverse_blocks.1 = (f32[6,5,2,64,256]{4,3,2,1,0:T(8,128)}, f32[6,2,64,256]{3,2,1,0:T(8,128)}) custom-call(f32[6,5,2,64,256]{4,3,2,1,0:T(8,128)} %bitcast_multiply_fusion.lp, f32[6,2,64,256]{3,2,1,0:T(8,128)} %bitcast.9), custom_call_target="tpu_custom_call" | custom-call | tf_op jit(solution)/shard_map/inverse_blocks/pallas_call | solution.py:370
  107.8 0.0 copy-start
  107.8 4.8 %select_bitcast_fusion = f32[1,6,5,2,64,256]{5,4,3,2,1,0:T(8,128)} fusion(f32[6,5,2,64,256]{4,3,2,1,0:T(8,128)} %get-tuple-element.4, pred[6]{0:T(512)(128)(4,1)S(1)} %fusion), kind=kLoop, calls=%fused_computation.1 | loop fusion | flops 983040 | bytes 7864326 | tf_op jit(solution)/shard_map/broadcast_in_dim | solution.py:426
  112.6 0.0 copy-done
  112.6 1.0 select_bitcast_fusion.1
  (1 shorter events, 0.0 us)
Async XLA Ops:
  107.8 4.8 %copy-start = (f32[6,2,64,256]{3,2,1,0:T(8,128)S(1)}, f32[6,2,64,256]{3,2,1,0:T(8,128)}, u32[]{:S(2)}) copy-start(f32[6,2,64,256]{3,2,1,0:T(8,128)} %get-tuple-element.5) | copy-start | bytes 2359300
where the time goes:
time: 114 us
  Pallas kernels  102 us (89%)
  other arithmetic  10.5 us (9%)
    pallas_call x1, Pallas kernels, inverse_blocks(): pl.pallas_call(kernel, out_shape=(jax.ShapeDtypeStruct((6, 5, 2, 64, W),...  102 us
    broadcast_in_dim x2, other arithmetic, body(): return (panel[None], diag[None])  5.77 us
    mul x1, other arithmetic, body(): masked = lower_panel[0] * structure[0].astype(F32)[:, :, None, None, None]  4.57 us

commit v1 on v0

v1 whole, which is shorter than its diff:
```python
import functools

import jax
import jax.numpy as jnp
from jax import lax
from jax.experimental import pallas as pl
from jax.experimental.pallas import tpu as pltpu
from jax.sharding import PartitionSpec as P

LEVELS = 6
MESH = pl.DeviceIdType.MESH
F32 = jnp.float32
BF16 = jnp.bfloat16
W = 256

AT = (None, 0, 1, 3, 6)
OUT = (0, 1, 3, 6, 10, 15)
X_AT = (None, 1, 3)
D_AT = (0, 2, 5)


def split(x):
    high = x.astype(BF16)
    return high, (x - high.astype(F32)).astype(BF16)


def mm(a, b):
    return jnp.dot(a, b, preferred_element_type=F32)


def kernel(
    st, lp, dg, out,
    f012, f3, f4, f5, lv, gh, gl, xh1, xl1, xh3, xl3, xh4, xl4, xh, xl, rb1, rb2, rb3, rb4, lh, ll, pk, yo, zo, dl,
    p1r, s0, s1, s2, s3, s4, ys, yr, xs, xr, cs, cr, os, ls,
):
    row = lax.axis_index("row")
    col = lax.axis_index("col")
    core = lax.rem(col, 2)
    xpos = lax.rem(col // 2, 4)
    plane = (col // 8) * 8
    up, down = lax.rem(row + 1, 4), lax.rem(row + 3, 4)
    xup, xdown = lax.rem(xpos + 1, 4), lax.rem(xpos + 3, 4)
    xfar = lax.rem(xpos + 2, 4)
    to_row = lambda r: {"row": r, "col": col}
    to_x = lambda x: {"row": row, "col": plane + 2 * x + core}
    other = {"row": row, "col": col + 1 - 2 * core}
    rbs = (None, rb1, rb2, rb3, rb4)
    my_rows = pl.ds(pl.multiple_of(row * 64, 64), 64)

    def is_home(d):
        return lax.rem(col, 2 ** (5 - d)) == 0

    def tell(device):
        pl.semaphore_signal(pltpu.get_barrier_semaphore(), inc=1, device_id=device, device_id_type=MESH)

    for device in (other, to_row(up), to_row(down), to_x(xup), to_x(xdown)):
        tell(device)
    for d in range(5):
        @pl.when(jnp.logical_not(is_home(d)))
        def _():
            size = 2 ** (5 - d)
            tell({"row": row, "col": (col // size) * size})

    loads = [pltpu.make_async_copy(lp.at[5], f5.at[:, :, row], ls.at[5])]
    for d in range(1, 5):
        loads.append(pltpu.make_async_copy(lp.at[d, 0:d], lv.at[AT[d] : AT[d] + d], ls.at[d]))
    d_leaf = pltpu.make_async_copy(dg.at[5], dl.at[0], ls.at[0])
    d_root = pltpu.make_async_copy(dg.at[0], dl.at[1], ls.at[6])
    for copy in loads + [d_leaf, d_root]:
        copy.start()
    loads[0].wait()
    for a in range(5):
        f5[a, :, row] = f5[a, :, row] * st[25 + a].astype(F32)
    for d in range(1, 5):
        loads[d].wait()
        for a in range(d):
            lv[AT[d] + a] = lv[AT[d] + a] * st[5 * d + a].astype(F32)

    callers = 5
    for d in range(5):
        callers = callers + is_home(d).astype(jnp.int32) * (2 ** (5 - d) - 1)
    pl.semaphore_wait(pltpu.get_barrier_semaphore(), callers)

    def remote(src, dst, send, recv, device):
        return pltpu.make_async_remote_copy(
            src_ref=src, dst_ref=dst, send_sem=send, recv_sem=recv, device_id=device, device_id_type=MESH
        )

    def pieces(d, j):
        kk = lax.rem(j, 2)
        mine = lv.at[AT[d] : AT[d] + d] if d else None
        if d <= 2:
            xx = lax.rem(j // 2, 4)
            part = pl.ds(pl.multiple_of(lax.rem(j, 8) * 8, 8), 8)
            out = [(dg.at[d, :, part], f012.at[D_AT[d], :, row, xx, kk])]
            if d:
                out.append((mine.at[:, :, part], f012.at[X_AT[d] : X_AT[d] + d, :, row, xx, kk]))
            return out
        part = pl.ds(pl.multiple_of(kk * 32, 32), 32)
        buf = f3 if d == 3 else f4
        return [
            (dg.at[d, :, part], buf.at[d, :, row, kk]),
            (mine.at[:, :, part], buf.at[0:d, :, row, kk]),
        ]

    sends = (s0, s1, s2, s3, s4)

    def home_copy(d, i, j):
        src, dst = pieces(d, j)[i]
        return remote(src, dst, sends[d].at[j - 1, i], p1r.at[d, i], {"row": row, "col": col + j})

    def n_pieces(d):
        return 2 if d else 1

    def home_start(d):
        @pl.when(is_home(d))
        def _():
            for i, (src, dst) in enumerate(pieces(d, 0)):
                pltpu.make_async_copy(src, dst, p1r.at[d, i]).start()

            def step(j, carry):
                for i in range(n_pieces(d)):
                    home_copy(d, i, j).start()
                return carry

            lax.fori_loop(1, 2 ** (5 - d), step, 0)

    def home_finish(d):
        @pl.when(is_home(d))
        def _():
            def step(j, carry):
                for i in range(n_pieces(d)):
                    home_copy(d, i, j).wait_send()
                return carry

            lax.fori_loop(1, 2 ** (5 - d), step, 0)

    def piece_wait(d):
        for i, (_, dst) in enumerate(pieces(d, lax.rem(col, 8))):
            pltpu.make_async_copy(dst, dst, p1r.at[d, i]).wait()

    def y_slice(n, r, half=None):
        h = slice(None) if half is None else half
        if n < 2:
            return f012.at[3 * n : 3 * n + 3, h, r, xpos, core]
        if n == 2:
            return f3.at[:, h, r, core]
        if n == 3:
            return f4.at[:, h, r, core]
        return f5.at[n - 4, h, r]

    def y_copy(n, q):
        if q == 0:
            ref, device = y_slice(n, row), up
        elif q == 1:
            ref, device = y_slice(n, row), down
        elif q == 2:
            ref, device = y_slice(n, down, 0), up
        else:
            ref, device = y_slice(n, up, 1), down
        return remote(ref, ref, ys.at[n, q], yr.at[n, q], to_row(device))

    def y_first(n):
        y_copy(n, 0).start()
        y_copy(n, 1).start()

    def y_forward(n):
        y_copy(n, 0).wait_recv()
        y_copy(n, 2).start()
        y_copy(n, 1).wait_recv()
        y_copy(n, 3).start()

    def y_done(n):
        y_copy(n, 2).wait_recv()
        y_copy(n, 3).wait_recv()

    def x_copy(c, q):
        blocks = f012.at[3 * c : 3 * c + 3]
        if q == 0:
            ref, device = blocks.at[:, :, :, xpos, core], xup
        elif q == 1:
            ref, device = blocks.at[:, :, :, xpos, core], xdown
        elif q == 2:
            ref, device = blocks.at[:, 0, :, xdown, core], xup
        else:
            ref, device = blocks.at[:, 1, :, xup, core], xdown
        return remote(ref, ref, xs.at[c, q], xr.at[c, q], to_x(device))

    def core_copy(q):
        if q < 8:
            ref = f012.at[3 * (q // 4) : 3 * (q // 4) + 3, :, :, (xpos, xdown, xup, xfar)[q % 4], core]
        elif q == 8:
            ref = f3.at[:, :, :, core]
        else:
            ref = f4.at[:, :, :, core]
        return remote(ref, ref, cs.at[q], cr.at[q], other)

    def x_first(c):
        y_done(c)
        x_copy(c, 0).start()
        x_copy(c, 1).start()
        core_copy(4 * c).start()

    def x_forward(c):
        x_copy(c, 0).wait_recv()
        x_copy(c, 2).start()
        core_copy(4 * c + 1).start()
        x_copy(c, 1).wait_recv()
        x_copy(c, 3).start()
        core_copy(4 * c + 2).start()

    def x_done(c):
        x_copy(c, 2).wait_recv()
        x_copy(c, 3).wait_recv()
        core_copy(4 * c + 3).start()

    def core_done(c):
        for q in range(4):
            core_copy(4 * c + q).wait_recv()

    for d in (0, 1, 2, 4, 3):
        home_start(d)
    y_first(4)
    piece_wait(0)
    piece_wait(1)
    y_first(0)
    piece_wait(2)
    y_first(1)
    y_first(5)
    y_forward(0)
    y_forward(1)
    piece_wait(4)
    y_first(3)
    x_first(0)
    x_first(1)
    piece_wait(3)
    y_first(2)
    y_forward(4)
    y_forward(5)
    y_first(6)
    x_forward(0)
    y_forward(3)
    x_done(0)
    x_forward(1)
    y_forward(2)
    y_first(7)
    y_first(8)
    d_root.wait()
    root_out = pltpu.make_async_copy(dl.at[1], out.at[0], os.at[0])
    root_out.start()

    def block(d, a, part):
        if d <= 2:
            return f012[X_AT[d] + a, part].reshape(W, W)
        if d == 3:
            return f3[a, part].reshape(W, W)
        if d == 4:
            return f4[a, part].reshape(W, W)
        return f5[a, part].reshape(W, W)

    def d_block(d, part):
        if d <= 2:
            return f012[D_AT[d], part].reshape(W, W)
        return (f3 if d == 3 else f4)[d, part].reshape(W, W)

    def put(high, low, rows, cols, real, imag):
        for m, value in enumerate((real, imag, real + imag)):
            h, l = split(value)
            high[m, rows, cols] = h
            low[m, rows, cols] = l

    xbufs = (None, (xh1, xl1), (xh1, xl1), (xh3, xl3), (xh4, xl4), (xh, xl))

    def prepare(d):
        high, low = xbufs[d]

        def step(f, carry):
            rows = pl.ds(pl.multiple_of(f * W, W), W)
            a = d - 1 - f
            put(high, low, rows, slice(None), block(d, a, 0), block(d, a, 1))
            return carry

        lax.fori_loop(0, d, step, 0)

    def three(high, low, rows, depth):
        x_high, x_low = xbufs[depth // W]
        out = []
        for m in range(3):
            a_high = high[m, rows, 0:depth]
            b_high = x_high[m, 0:depth, :]
            acc = mm(a_high, b_high) + mm(a_high, x_low[m, 0:depth, :])
            out.append(acc + mm(low[m, rows, 0:depth], b_high))
        return out[1] - out[0], out[0] + out[1] - out[2]


    outs = []

    def level(d):
        rb = rbs[d]
        depth = d * W
        new = slice(depth, depth + W)

        def step(e, carry):
            at = pl.ds(pl.multiple_of(e * W, W), W)
            real, imag = three(gh, gl, at, depth)
            last = (e == d).astype(F32)
            real = real + last * d_block(d, 0)
            imag = imag + last * d_block(d, 1)
            slot = jnp.where(e == d, d, d - 1 - e)
            rb[slot, 0] = real
            rb[slot, 1] = imag
            put(gh, gl, at, new, real, imag)
            put(gh, gl, new, at, real.T, imag.T)
            return carry

        lax.fori_loop(0, d + 1, step, 0)
        copies = [
            pltpu.make_async_copy(rb.at[:, :, my_rows], out.at[OUT[d] : OUT[d] + d + 1], os.at[d]),
        ]
        for copy in copies:
            copy.start()
        outs.extend(copies)

    y_done(2)
    core_copy(8).start()
    core_done(0)
    put(gh, gl, slice(0, W), slice(0, W), d_block(0, 0), d_block(0, 1))
    prepare(1)
    level(1)
    x_done(1)
    y_done(3)
    core_copy(9).start()
    y_forward(6)
    core_copy(8).wait_recv()
    prepare(3)
    core_done(1)
    prepare(2)
    level(2)
    y_forward(7)
    core_copy(9).wait_recv()
    level(3)
    y_forward(8)
    prepare(4)
    level(4)
    for n in range(4, 9):
        y_done(n)

    prepare(5)

    def pick(x):
        out = x[:, 0:64]
        for r in range(1, 4):
            out = jnp.where(row == r, x[:, 64 * r : 64 * r + 64], out)
        return out

    def pack(f, carry):
        rows = pl.ds(pl.multiple_of(f * W, W), W)
        real, imag = pick(block(5, 4 - f, 0)), pick(block(5, 4 - f, 1))
        rh, rl = split(real)
        ih, il = split(imag)
        pk[rows, :] = jnp.concatenate([v.astype(F32) for v in (rh, ih, rl, il)], axis=1).astype(BF16)
        return carry

    lax.fori_loop(0, 5, pack, 0)

    def columns(e, carry):
        at = pl.ds(pl.multiple_of(e * W, W), W)
        p = pk[...]
        a = mm(gh[0, at, :], p) + mm(gl[0, at, :], p)
        b = mm(gh[1, at, :], p) + mm(gl[1, at, :], p)
        real = b[:, 64:128] + b[:, 192:256] - a[:, 0:64] - a[:, 128:192]
        imag = -(a[:, 64:128] + a[:, 192:256] + b[:, 0:64] + b[:, 128:192])
        flipped = jnp.concatenate([real, imag], axis=1).T
        put(lh, ll, slice(320, 384), at, flipped[0:64], flipped[64:128])
        mine = pl.ds(pl.multiple_of(e * W + row * 64, 64), 64)
        to = pl.ds(pl.multiple_of(e * 64, 64), 64)
        for m in range(3):
            lh[m, to, :] = gh[m, mine, :]
            ll[m, to, :] = gl[m, mine, :]
        return carry

    lax.fori_loop(0, 5, columns, 0)
    real, imag = three(lh, ll, slice(0, 384), 5 * W)
    for e in range(5):
        yo[4 - e, 0] = real[64 * e : 64 * e + 64]
        yo[4 - e, 1] = imag[64 * e : 64 * e + 64]
    d_leaf.wait()
    zo[0] = dl[0, 0] + real[320:384]
    zo[1] = dl[0, 1] + imag[320:384]
    copies = [
        pltpu.make_async_copy(yo, out.at[15:20], os.at[5]),
        pltpu.make_async_copy(zo, out.at[20], os.at[6]),
    ]
    for copy in copies:
        copy.start()

    for d in range(5):
        home_finish(d)
    for n in range(9):
        for q in range(4):
            y_copy(n, q).wait_send()
    for c in range(2):
        for q in range(4):
            x_copy(c, q).wait_send()
    for q in range(10):
        core_copy(q).wait_send()
    for copy in [root_out] + outs + copies:
        copy.wait()


def inverse_blocks(st, lp, dg):
    dma = pltpu.SemaphoreType.DMA
    vmem = pltpu.VMEM
    side = 5 * W
    any_spec = pl.BlockSpec(memory_space=pl.ANY)
    return pl.pallas_call(
        kernel,
        out_shape=jax.ShapeDtypeStruct((21, 2, 64, W), F32),
        in_specs=[pl.BlockSpec(memory_space=pltpu.SMEM), any_spec, any_spec],
        out_specs=any_spec,
        scratch_shapes=[
            vmem((6, 2, 4, 4, 2, 8, W), F32),
            vmem((4, 2, 4, 2, 32, W), F32),
            vmem((5, 2, 4, 2, 32, W), F32),
            vmem((5, 2, 4, 64, W), F32),
            vmem((10, 2, 64, W), F32),
            vmem((3, side, side), BF16),
            vmem((3, side, side), BF16),
            vmem((3, 2 * W, W), BF16),
            vmem((3, 2 * W, W), BF16),
            vmem((3, 3 * W, W), BF16),
            vmem((3, 3 * W, W), BF16),
            vmem((3, 4 * W, W), BF16),
            vmem((3, 4 * W, W), BF16),
            vmem((3, side, W), BF16),
            vmem((3, side, W), BF16),
            vmem((2, 2, W, W), F32),
            vmem((3, 2, W, W), F32),
            vmem((4, 2, W, W), F32),
            vmem((5, 2, W, W), F32),
            vmem((3, 384, side), BF16),
            vmem((3, 384, side), BF16),
            vmem((side, W), BF16),
            vmem((5, 2, 64, W), F32),
            vmem((2, 64, W), F32),
            vmem((2, 2, 64, W), F32),
            dma((5, 2)),
            dma((31, 1)),
            dma((15, 2)),
            dma((7, 2)),
            dma((3, 2)),
            dma((1, 2)),
            dma((9, 4)),
            dma((9, 4)),
            dma((2, 4)),
            dma((2, 4)),
            dma((10,)),
            dma((10,)),
            dma((7,)),
            dma((7,)),
        ],
        compiler_params=pltpu.CompilerParams(
            vmem_limit_bytes=66_000_000, has_side_effects=True, collective_id=1
        ),
        name="inverse_blocks",
    )(st, lp, dg)


def spread(src, panel, diag, buf, zero, rs, ws):
    col = lax.axis_index("col")

    def active(d):
        return lax.rem(col, 2 ** (5 - d)) == 0

    def read(d):
        at = slice(OUT[d], OUT[d] + d + 1)
        return pltpu.make_async_copy(src.at[at], buf.at[at], rs.at[d])

    for d in range(LEVELS):
        @pl.when(active(d))
        def _():
            read(d).start()

    zero[...] = jnp.zeros_like(zero)
    for d in range(5):
        pltpu.make_async_copy(zero.at[0 : 5 - d], panel.at[d, d:5], ws.at[0, d]).start()

    def write(d, real):
        blocks = buf if real else zero
        at = OUT[d] if real else 0
        out = [pltpu.make_async_copy(blocks.at[at + d if real else 0], diag.at[d], ws.at[1, d])]
        if d:
            out.append(pltpu.make_async_copy(blocks.at[at : at + d], panel.at[d, 0:d], ws.at[2, d]))
        return out

    for d in range(5):
        @pl.when(jnp.logical_not(active(d)))
        def _():
            for copy in write(d, False):
                copy.start()

    for d in range(LEVELS):
        @pl.when(active(d))
        def _():
            read(d).wait()
            for copy in write(d, True):
                copy.start()

    for d in range(5):
        pltpu.make_async_copy(zero.at[0 : 5 - d], panel.at[d, d:5], ws.at[0, d]).wait()
    for d in range(LEVELS):
        for copy in write(d, True):
            copy.wait()


def spread_out(blocks):
    dma = pltpu.SemaphoreType.DMA
    any_spec = pl.BlockSpec(memory_space=pl.ANY)
    return pl.pallas_call(
        spread,
        out_shape=(
            jax.ShapeDtypeStruct((6, 5, 2, 64, W), F32),
            jax.ShapeDtypeStruct((6, 2, 64, W), F32),
        ),
        in_specs=[any_spec],
        out_specs=(any_spec, any_spec),
        scratch_shapes=[
            pltpu.VMEM((21, 2, 64, W), F32),
            pltpu.VMEM((5, 2, 64, W), F32),
            dma((6,)),
            dma((3, 6)),
        ],
        name="spread_out",
    )(blocks)


def body(lower_panel, diag_inverse, structure):
    blocks = inverse_blocks(structure.reshape(30), lower_panel[0], diag_inverse[0])
    panel, diag = spread_out(blocks)
    return panel[None], diag[None]


def solution(mesh):
    in_specs = (
        P("col", None, None, None, "row", None),
        P("col", None, None, "row", None),
        P("col", None, None),
    )
    out_specs = (P("col", None, None, None, "row", None), P("col", None, None, "row", None))
    return jax.shard_map(body, mesh=mesh, in_specs=in_specs, out_specs=out_specs, check_vma=False)
```

time: 114 us -> 89.8 us (0.79)
  the two profiles are of different devices: /device:TPU:1 before, /device:TPU:5 now
where the time goes in v1:
time: 89.8 us; the launch traced here: 89.5 us
  Pallas kernels  87.5 us (97%)
  local copies, waits for them, and re-layouts  1.36 us (2%)
    pallas_call x1, Pallas kernels, inverse_blocks(): pl.pallas_call(kernel, out_shape=jax.ShapeDtypeStruct((21, 2, 64, W), F32...  84.7 us
    pallas_call x1, Pallas kernels, spread_out(): pl.pallas_call(spread, out_shape=(jax.ShapeDtypeStruct((6, 5, 2, 64, W),...  2.88 us

profile of v1, /device:TPU:5, one launch (start us, length us, event | category | flops | bytes accessed | tf_op | source)
XLA Modules:
  0.0 89.5 jit_solution(18223217486353651526)
XLA Ops:
  0.6 0.8 copy.6
  1.4 0.6 reshape.7.st
  2.0 84.7 %inverse_blocks.1.src = f32[21,2,64,256]{3,2,1,0:T(8,128)} custom-call(s32[30]{0:T(128)} %reshape.7.st, f32[6,5,2,64,256]{4,3,2,1,0:T(8,128)} %bitcast.4, f32[6,2,64,256]{3,2,1,0:T(8,128)} %bitcast.5), custom_call_target="tpu_custom_call" | custom-call | tf_op jit(solution)/shard_map/inverse_blocks/pallas_call | solution.py:416
  86.7 2.9 %spread_out.1 = (f32[6,5,2,64,256]{4,3,2,1,0:T(8,128)}, f32[6,2,64,256]{3,2,1,0:T(8,128)}) custom-call(f32[21,2,64,256]{3,2,1,0:T(8,128)} %inverse_blocks.1.src), custom_call_target="tpu_custom_call" | custom-call | tf_op jit(solution)/shard_map/spread_out/pallas_call | solution.py:519

commit v2 on v1

--- a/solution.py
+++ b/solution.py
@@ -30,8 +30,8 @@
 
 def kernel(
     st, lp, dg, out,
-    f012, f3, f4, f5, lv, gh, gl, xh1, xl1, xh3, xl3, xh4, xl4, xh, xl, rb1, rb2, rb3, rb4, lh, ll, pk, yo, zo, dl,
-    p1r, s0, s1, s2, s3, s4, ys, yr, xs, xr, cs, cr, os, ls,
+    f012, f3, f4, f5, lv, xnh, xnl, xth, xtl, dnh, dnl, u, uh, ul, v, vh, vl, lh, ll, yo, no, dl,
+    p1r, s0, s1, s2, s3, s4, ys, yr, xs, xr, cs, cr, os, ls, ns, nr,
 ):
     row = lax.axis_index("row")
     col = lax.axis_index("col")
@@ -44,7 +44,6 @@
     to_row = lambda r: {"row": r, "col": col}
     to_x = lambda x: {"row": row, "col": plane + 2 * x + core}
     other = {"row": row, "col": col + 1 - 2 * core}
-    rbs = (None, rb1, rb2, rb3, rb4)
     my_rows = pl.ds(pl.multiple_of(row * 64, 64), 64)
 
     def is_home(d):
@@ -70,11 +69,11 @@
         copy.start()
     loads[0].wait()
     for a in range(5):
-        f5[a, :, row] = f5[a, :, row] * st[25 + a].astype(F32)
+        f5[a, :, row] = f5[a, :, row] * st[0, 5, a].astype(F32)
     for d in range(1, 5):
         loads[d].wait()
         for a in range(d):
-            lv[AT[d] + a] = lv[AT[d] + a] * st[5 * d + a].astype(F32)
+            lv[AT[d] + a] = lv[AT[d] + a] * st[0, d, a].astype(F32)
 
     callers = 5
     for d in range(5):
@@ -220,6 +219,173 @@
 
     for d in (0, 1, 2, 4, 3):
         home_start(d)
+    def block(d, a, part):
+        if d <= 2:
+            return f012[X_AT[d] + a, part].reshape(W, W)
+        if d == 3:
+            return f3[a, part].reshape(W, W)
+        return f4[a, part].reshape(W, W)
+
+    def d_block(d, part):
+        if d <= 2:
+            return f012[D_AT[d], part].reshape(W, W)
+        return (f3 if d == 3 else f4)[d, part].reshape(W, W)
+
+    def put(high, low, i, real, imag):
+        for m, value in enumerate((real, imag, real + imag)):
+            high[i, m], low[i, m] = split(value)
+
+    def at(f, e):
+        return f * (f - 1) // 2 + e
+
+    def prepare(d):
+        def step(e, carry):
+            real, imag = block(d, d - 1 - e, 0), block(d, d - 1 - e, 1)
+            put(xnh, xnl, at(d, 0) + e, real, imag)
+            put(xth, xtl, at(d, 0) + e, real.T, imag.T)
+            return carry
+
+        lax.fori_loop(0, d, step, 0)
+        put(dnh, dnl, d, d_block(d, 0), d_block(d, 1))
+
+    def three(lefts, rights):
+        out = []
+        for m in range(3):
+            a_high, a_low = lefts(m)
+            b_high, b_low = rights(m)
+            out.append(mm(a_high, b_high) + mm(a_high, b_low) + mm(a_low, b_high))
+        return out[0] - out[1], out[2] - out[0] - out[1]
+
+    def product(high, low, i, bh, bl, j):
+        return three(lambda m: (high[i, m], low[i, m]), lambda m: (bh[j, m], bl[j, m]))
+
+    def forward(f, x, xh, xl):
+        put(xh, xl, f, x[f, 0], x[f, 1])
+
+        def step(e, carry):
+            real, imag = product(xnh, xnl, at(f, e), xh, xl, f)
+            x[e, 0] = x[e, 0] - real
+            x[e, 1] = x[e, 1] - imag
+            return carry
+
+        lax.fori_loop(0, f, step, 0)
+
+    def scale(e, x, xh, xl):
+        real, imag = product(dnh, dnl, e, xh, xl, e)
+        x[e, 0] = real
+        x[e, 1] = imag
+
+    def backward(e, d, x, xh, xl):
+        put(xh, xl, e, x[e, 0], x[e, 1])
+
+        def step(f, carry):
+            real, imag = product(xth, xtl, at(f, e), xh, xl, e)
+            x[f, 0] = x[f, 0] - real
+            x[f, 1] = x[f, 1] - imag
+            return carry
+
+        lax.fori_loop(e + 1, d, step, 0)
+
+    odd = lax.rem(col, 2) == 1
+    second = lax.rem(col, 4) == 2
+    whole = lax.rem(col, 8) == 0
+    first = jnp.where(odd, 4, jnp.where(second, 3, jnp.where(whole, jnp.where(lax.rem(col, 16) == 0, 1, 2), 0)))
+    last = jnp.where(odd, 5, jnp.where(second, 4, jnp.where(whole, 3, 0)))
+
+    def node_out(d, i):
+        home = jnp.where(d == 4, col - 1, col - 2)
+        src, dst = no.at[lax.rem(d, 2), i], out.at[d * (d + 1) // 2 + i]
+        far = remote(src, dst, ns.at[d, i], nr.at[d, i], {"row": row, "col": home})
+        near = pltpu.make_async_copy(src, dst, ns.at[d, i])
+        return far, near
+
+    def node(d, carry):
+        def load(e, c):
+            for m in range(2):
+                i = at(d, e)
+                v[e, m] = xnh[i, m].astype(F32) + xnl[i, m].astype(F32)
+            return c
+
+        def forwards(i, c):
+            forward(d - 1 - i, v, vh, vl)
+            return c
+
+        def scales(e, c):
+            scale(e, v, vh, vl)
+            return c
+
+        def backwards(e, c):
+            backward(e, d, v, vh, vl)
+            return c
+
+        lax.fori_loop(0, d, load, 0)
+        lax.fori_loop(0, d, forwards, 0)
+        lax.fori_loop(0, d, scales, 0)
+        lax.fori_loop(0, d, backwards, 0)
+
+        side = lax.rem(d, 2)
+        real = (dnh[d, 0, my_rows, :].astype(F32) + dnl[d, 0, my_rows, :].astype(F32))
+        imag = (dnh[d, 1, my_rows, :].astype(F32) + dnl[d, 1, my_rows, :].astype(F32))
+
+        def diagonal(e, c):
+            i = at(d, e)
+            r, m = three(
+                lambda m: (xth[i, m, my_rows, :], xtl[i, m, my_rows, :]), lambda m: (vh[e, m], vl[e, m])
+            )
+            for p in range(2):
+                no[side, d - 1 - e, p] = -v[e, p, my_rows, :]
+            return c[0] + r, c[1] + m
+
+        real, imag = lax.fori_loop(0, d, diagonal, (real, imag))
+        no[side, d, 0] = real
+        no[side, d, 1] = imag
+
+        def send(i, c):
+            far, near = node_out(d, i)
+
+            @pl.when(d >= 3)
+            def _():
+                far.start()
+
+            @pl.when(d < 3)
+            def _():
+                near.start()
+
+            return c
+
+        lax.fori_loop(0, d + 1, send, 0)
+        return carry
+
+    def node_finish(d, carry):
+        def finish(i, c):
+            far, near = node_out(d, i)
+
+            @pl.when(d >= 3)
+            def _():
+                far.wait_send()
+
+            @pl.when(d < 3)
+            def _():
+                near.wait()
+
+            return c
+
+        lax.fori_loop(0, d + 1, finish, 0)
+        return carry
+
+    def pick(x):
+        out = x[:, 0:64]
+        for r in range(1, 4):
+            out = jnp.where(row == r, x[:, 64 * r : 64 * r + 64], out)
+        return out
+
+    def leaf_block(a):
+        real, imag = f5[a, 0].reshape(W, W), f5[a, 1].reshape(W, W)
+        u[4 - a, 0] = u[4 - a, 0] + real
+        u[4 - a, 1] = u[4 - a, 1] + imag
+        flipped = jnp.concatenate([pick(real), pick(imag)], axis=1).T
+        put(lh, ll, 4 - a, flipped[0:64], flipped[64:128])
+
     y_first(4)
     piece_wait(0)
     piece_wait(1)
@@ -235,164 +401,72 @@
     x_first(1)
     piece_wait(3)
     y_first(2)
+    y_first(6)
     y_forward(4)
     y_forward(5)
-    y_first(6)
     x_forward(0)
     y_forward(3)
     x_done(0)
     x_forward(1)
-    y_forward(2)
     y_first(7)
     y_first(8)
+    y_forward(2)
     d_root.wait()
     root_out = pltpu.make_async_copy(dl.at[1], out.at[0], os.at[0])
     root_out.start()
-
-    def block(d, a, part):
-        if d <= 2:
-            return f012[X_AT[d] + a, part].reshape(W, W)
-        if d == 3:
-            return f3[a, part].reshape(W, W)
-        if d == 4:
-            return f4[a, part].reshape(W, W)
-        return f5[a, part].reshape(W, W)
-
-    def d_block(d, part):
-        if d <= 2:
-            return f012[D_AT[d], part].reshape(W, W)
-        return (f3 if d == 3 else f4)[d, part].reshape(W, W)
-
-    def put(high, low, rows, cols, real, imag):
-        for m, value in enumerate((real, imag, real + imag)):
-            h, l = split(value)
-            high[m, rows, cols] = h
-            low[m, rows, cols] = l
-
-    xbufs = (None, (xh1, xl1), (xh1, xl1), (xh3, xl3), (xh4, xl4), (xh, xl))
-
-    def prepare(d):
-        high, low = xbufs[d]
-
-        def step(f, carry):
-            rows = pl.ds(pl.multiple_of(f * W, W), W)
-            a = d - 1 - f
-            put(high, low, rows, slice(None), block(d, a, 0), block(d, a, 1))
-            return carry
-
-        lax.fori_loop(0, d, step, 0)
-
-    def three(high, low, rows, depth):
-        x_high, x_low = xbufs[depth // W]
-        out = []
-        for m in range(3):
-            a_high = high[m, rows, 0:depth]
-            b_high = x_high[m, 0:depth, :]
-            acc = mm(a_high, b_high) + mm(a_high, x_low[m, 0:depth, :])
-            out.append(acc + mm(low[m, rows, 0:depth], b_high))
-        return out[1] - out[0], out[0] + out[1] - out[2]
-
-
-    outs = []
-
-    def level(d):
-        rb = rbs[d]
-        depth = d * W
-        new = slice(depth, depth + W)
-
-        def step(e, carry):
-            at = pl.ds(pl.multiple_of(e * W, W), W)
-            real, imag = three(gh, gl, at, depth)
-            last = (e == d).astype(F32)
-            real = real + last * d_block(d, 0)
-            imag = imag + last * d_block(d, 1)
-            slot = jnp.where(e == d, d, d - 1 - e)
-            rb[slot, 0] = real
-            rb[slot, 1] = imag
-            put(gh, gl, at, new, real, imag)
-            put(gh, gl, new, at, real.T, imag.T)
-            return carry
-
-        lax.fori_loop(0, d + 1, step, 0)
-        copies = [
-            pltpu.make_async_copy(rb.at[:, :, my_rows], out.at[OUT[d] : OUT[d] + d + 1], os.at[d]),
-        ]
-        for copy in copies:
-            copy.start()
-        outs.extend(copies)
-
-    y_done(2)
-    core_copy(8).start()
-    core_done(0)
-    put(gh, gl, slice(0, W), slice(0, W), d_block(0, 0), d_block(0, 1))
-    prepare(1)
-    level(1)
-    x_done(1)
+    u[...] = jnp.zeros_like(u)
     y_done(3)
     core_copy(9).start()
     y_forward(6)
+    y_done(4)
+    leaf_block(0)
+    y_done(5)
+    leaf_block(1)
+    core_copy(9).wait_recv()
+    prepare(4)
+    y_done(2)
+    core_copy(8).start()
+    x_done(1)
+    forward(4, u, uh, ul)
+    y_forward(7)
     core_copy(8).wait_recv()
     prepare(3)
+    core_done(0)
+    put(dnh, dnl, 0, d_block(0, 0), d_block(0, 1))
+    prepare(1)
+    y_forward(8)
+    forward(3, u, uh, ul)
     core_done(1)
     prepare(2)
-    level(2)
-    y_forward(7)
-    core_copy(9).wait_recv()
-    level(3)
-    y_forward(8)
-    prepare(4)
-    level(4)
-    for n in range(4, 9):
-        y_done(n)
-
-    prepare(5)
-
-    def pick(x):
-        out = x[:, 0:64]
-        for r in range(1, 4):
-            out = jnp.where(row == r, x[:, 64 * r : 64 * r + 64], out)
-        return out
-
-    def pack(f, carry):
-        rows = pl.ds(pl.multiple_of(f * W, W), W)
-        real, imag = pick(block(5, 4 - f, 0)), pick(block(5, 4 - f, 1))
-        rh, rl = split(real)
-        ih, il = split(imag)
-        pk[rows, :] = jnp.concatenate([v.astype(F32) for v in (rh, ih, rl, il)], axis=1).astype(BF16)
-        return carry
-
-    lax.fori_loop(0, 5, pack, 0)
-
-    def columns(e, carry):
-        at = pl.ds(pl.multiple_of(e * W, W), W)
-        p = pk[...]
-        a = mm(gh[0, at, :], p) + mm(gl[0, at, :], p)
-        b = mm(gh[1, at, :], p) + mm(gl[1, at, :], p)
-        real = b[:, 64:128] + b[:, 192:256] - a[:, 0:64] - a[:, 128:192]
-        imag = -(a[:, 64:128] + a[:, 192:256] + b[:, 0:64] + b[:, 128:192])
-        flipped = jnp.concatenate([real, imag], axis=1).T
-        put(lh, ll, slice(320, 384), at, flipped[0:64], flipped[64:128])
-        mine = pl.ds(pl.multiple_of(e * W + row * 64, 64), 64)
-        to = pl.ds(pl.multiple_of(e * 64, 64), 64)
-        for m in range(3):
-            lh[m, to, :] = gh[m, mine, :]
-            ll[m, to, :] = gl[m, mine, :]
-        return carry
-
-    lax.fori_loop(0, 5, columns, 0)
-    real, imag = three(lh, ll, slice(0, 384), 5 * W)
+    y_done(6)
+    leaf_block(2)
+    forward(2, u, uh, ul)
+    lax.fori_loop(first, last, node, 0)
+    y_done(7)
+    leaf_block(3)
+    forward(1, u, uh, ul)
+    for e in range(1, 5):
+        scale(e, u, uh, ul)
+    y_done(8)
+    leaf_block(4)
+    put(uh, ul, 0, u[0, 0], u[0, 1])
+    scale(0, u, uh, ul)
     for e in range(5):
-        yo[4 - e, 0] = real[64 * e : 64 * e + 64]
-        yo[4 - e, 1] = imag[64 * e : 64 * e + 64]
+        backward(e, 5, u, uh, ul)
+    for e in range(5):
+        for p in range(2):
+            yo[4 - e, p] = -u[e, p, my_rows, :]
     d_leaf.wait()
-    zo[0] = dl[0, 0] + real[320:384]
-    zo[1] = dl[0, 1] + imag[320:384]
-    copies = [
-        pltpu.make_async_copy(yo, out.at[15:20], os.at[5]),
-        pltpu.make_async_copy(zo, out.at[20], os.at[6]),
-    ]
-    for copy in copies:
-        copy.start()
+    copies = [pltpu.make_async_copy(yo.at[0:5], out.at[15:20], os.at[1])]
+    copies[0].start()
+
+    def diagonal(e, c):
+        r, m = three(lambda m: (lh[e, m], ll[e, m]), lambda m: (uh[e, m], ul[e, m]))
+        return c[0] + r, c[1] + m
+
+    yo[5, 0], yo[5, 1] = lax.fori_loop(0, 5, diagonal, (dl[0, 0], dl[0, 1]))
+    copies.append(pltpu.make_async_copy(yo.at[5], out.at[20], os.at[2]))
+    copies[1].start()
 
     for d in range(5):
         home_finish(d)
@@ -404,14 +478,20 @@
             x_copy(c, q).wait_send()
     for q in range(10):
         core_copy(q).wait_send()
-    for copy in [root_out] + outs + copies:
+    lax.fori_loop(first, last, node_finish, 0)
+    for d in (3, 4):
+        @pl.when(is_home(d))
+        def _():
+            for i in range(d + 1):
+                blk = out.at[d * (d + 1) // 2 + i]
+                pltpu.make_async_copy(blk, blk, nr.at[d, i]).wait()
+    for copy in [root_out] + copies:
         copy.wait()
 
 
 def inverse_blocks(st, lp, dg):
     dma = pltpu.SemaphoreType.DMA
     vmem = pltpu.VMEM
-    side = 5 * W
     any_spec = pl.BlockSpec(memory_space=pl.ANY)
     return pl.pallas_call(
         kernel,
@@ -424,25 +504,15 @@
             vmem((5, 2, 4, 2, 32, W), F32),
             vmem((5, 2, 4, 64, W), F32),
             vmem((10, 2, 64, W), F32),
-            vmem((3, side, side), BF16),
-            vmem((3, side, side), BF16),
-            vmem((3, 2 * W, W), BF16),
-            vmem((3, 2 * W, W), BF16),
-            vmem((3, 3 * W, W), BF16),
-            vmem((3, 3 * W, W), BF16),
-            vmem((3, 4 * W, W), BF16),
-            vmem((3, 4 * W, W), BF16),
-            vmem((3, side, W), BF16),
-            vmem((3, side, W), BF16),
-            vmem((2, 2, W, W), F32),
-            vmem((3, 2, W, W), F32),
+            *[vmem((10, 3, W, W), BF16)] * 4,
+            *[vmem((5, 3, W, W), BF16)] * 2,
+            vmem((5, 2, W, W), F32),
+            *[vmem((5, 3, W, W), BF16)] * 2,
             vmem((4, 2, W, W), F32),
-            vmem((5, 2, W, W), F32),
-            vmem((3, 384, side), BF16),
-            vmem((3, 384, side), BF16),
-            vmem((side, W), BF16),
-            vmem((5, 2, 64, W), F32),
-            vmem((2, 64, W), F32),
+            *[vmem((4, 3, W, W), BF16)] * 2,
+            *[vmem((5, 3, 64, W), BF16)] * 2,
+            vmem((6, 2, 64, W), F32),
+            vmem((2, 5, 2, 64, W), F32),
             vmem((2, 2, 64, W), F32),
             dma((5, 2)),
             dma((31, 1)),
@@ -456,8 +526,10 @@
             dma((2, 4)),
             dma((10,)),
             dma((10,)),
+            dma((3,)),
             dma((7,)),
-            dma((7,)),
+            dma((5, 5)),
+            dma((5, 5)),
         ],
         compiler_params=pltpu.CompilerParams(
             vmem_limit_bytes=66_000_000, has_side_effects=True, collective_id=1
@@ -535,7 +607,7 @@
 
 
 def body(lower_panel, diag_inverse, structure):
-    blocks = inverse_blocks(structure.reshape(30), lower_panel[0], diag_inverse[0])
+    blocks = inverse_blocks(structure, lower_panel[0], diag_inverse[0])
     panel, diag = spread_out(blocks)
     return panel[None], diag[None]
 

time: 89.8 us -> 92.1 us (1.026)
  Pallas kernels: 87.5 us -> 89.8 us
    pallas_call x1, Pallas kernels: 84.7 us -> 87 us  [inverse_blocks(): pl.pallas_call(kernel, out_shape=jax.ShapeDtypeStruct((21, 2, 64, W), F32...]
where the time goes in v2:
time: 92.1 us; the launch traced here: 91.8 us
  Pallas kernels  89.8 us (98%)
  local copies, waits for them, and re-layouts  1.36 us (1%)
    pallas_call x1, Pallas kernels, inverse_blocks(): pl.pallas_call(kernel, out_shape=jax.ShapeDtypeStruct((21, 2, 64, W), F32...  87 us
    pallas_call x1, Pallas kernels, spread_out(): pl.pallas_call(spread, out_shape=(jax.ShapeDtypeStruct((6, 5, 2, 64, W),...  2.88 us

profile of v2, /device:TPU:5, one launch (start us, length us, event | category | flops | bytes accessed | tf_op | source)
XLA Modules:
  0.0 91.8 jit_solution(2351230603094549625)
XLA Ops:
  0.6 1.4 %copy.5.st = s32[1,6,5]{2,1,0:T(8,128)} copy(s32[1,6,5]{1,0,2:T(1,128)} %param.5) | data formatting | bytes 240 | tf_op args[2]
  2.0 87.0 %inverse_blocks.1.src = f32[21,2,64,256]{3,2,1,0:T(8,128)} custom-call(s32[1,6,5]{2,1,0:T(8,128)} %copy.5.st, f32[6,5,2,64,256]{4,3,2,1,0:T(8,128)} %bitcast.4, f32[6,2,64,256]{3,2,1,0:T(8,128)} %bitcast.5), custom_call_target="tpu_custom_call" | custom-call | tf_op jit(solution)/shard_map/inverse_blocks/pallas_call | solution.py:496
  89.0 2.9 %spread_out.1 = (f32[6,5,2,64,256]{4,3,2,1,0:T(8,128)}, f32[6,2,64,256]{3,2,1,0:T(8,128)}) custom-call(f32[21,2,64,256]{3,2,1,0:T(8,128)} %inverse_blocks.1.src), custom_call_target="tpu_custom_call" | custom-call | tf_op jit(solution)/shard_map/spread_out/pallas_call | solution.py:591

commit v3 on v2

--- a/solution.py
+++ b/solution.py
@@ -268,7 +268,7 @@
             x[e, 1] = x[e, 1] - imag
             return carry
 
-        lax.fori_loop(0, f, step, 0)
+        lax.fori_loop(0, f, step, 0, unroll=isinstance(f, int))
 
     def scale(e, x, xh, xl):
         real, imag = product(dnh, dnl, e, xh, xl, e)
@@ -284,7 +284,7 @@
             x[f, 1] = x[f, 1] - imag
             return carry
 
-        lax.fori_loop(e + 1, d, step, 0)
+        lax.fori_loop(e + 1, d, step, 0, unroll=isinstance(d, int))
 
     odd = lax.rem(col, 2) == 1
     second = lax.rem(col, 4) == 2
@@ -292,86 +292,51 @@
     first = jnp.where(odd, 4, jnp.where(second, 3, jnp.where(whole, jnp.where(lax.rem(col, 16) == 0, 1, 2), 0)))
     last = jnp.where(odd, 5, jnp.where(second, 4, jnp.where(whole, 3, 0)))
 
-    def node_out(d, i):
-        home = jnp.where(d == 4, col - 1, col - 2)
-        src, dst = no.at[lax.rem(d, 2), i], out.at[d * (d + 1) // 2 + i]
-        far = remote(src, dst, ns.at[d, i], nr.at[d, i], {"row": row, "col": home})
-        near = pltpu.make_async_copy(src, dst, ns.at[d, i])
-        return far, near
-
-    def node(d, carry):
-        def load(e, c):
+    def node_copy(d, i):
+        src, dst = no.at[d % 2, i], out.at[OUT[d] + i]
+        if d >= 3:
+            home = {"row": row, "col": col - (1 if d == 4 else 2)}
+            return remote(src, dst, ns.at[d, i], nr.at[d, i], home)
+        return pltpu.make_async_copy(src, dst, ns.at[d, i])
+
+    def node(d):
+        for e in range(d):
             for m in range(2):
-                i = at(d, e)
-                v[e, m] = xnh[i, m].astype(F32) + xnl[i, m].astype(F32)
-            return c
-
-        def forwards(i, c):
-            forward(d - 1 - i, v, vh, vl)
-            return c
-
-        def scales(e, c):
+                v[e, m] = xnh[at(d, e), m].astype(F32) + xnl[at(d, e), m].astype(F32)
+        for f in range(d - 1, -1, -1):
+            forward(f, v, vh, vl)
+        for e in range(d):
             scale(e, v, vh, vl)
-            return c
-
-        def backwards(e, c):
+        for e in range(d):
             backward(e, d, v, vh, vl)
-            return c
-
-        lax.fori_loop(0, d, load, 0)
-        lax.fori_loop(0, d, forwards, 0)
-        lax.fori_loop(0, d, scales, 0)
-        lax.fori_loop(0, d, backwards, 0)
-
-        side = lax.rem(d, 2)
-        real = (dnh[d, 0, my_rows, :].astype(F32) + dnl[d, 0, my_rows, :].astype(F32))
-        imag = (dnh[d, 1, my_rows, :].astype(F32) + dnl[d, 1, my_rows, :].astype(F32))
-
-        def diagonal(e, c):
+        side = d % 2
+        real, imag = (dnh[d, m, my_rows, :].astype(F32) + dnl[d, m, my_rows, :].astype(F32) for m in range(2))
+        for e in range(d):
             i = at(d, e)
             r, m = three(
                 lambda m: (xth[i, m, my_rows, :], xtl[i, m, my_rows, :]), lambda m: (vh[e, m], vl[e, m])
             )
             for p in range(2):
                 no[side, d - 1 - e, p] = -v[e, p, my_rows, :]
-            return c[0] + r, c[1] + m
-
-        real, imag = lax.fori_loop(0, d, diagonal, (real, imag))
+            real, imag = real + r, imag + m
         no[side, d, 0] = real
         no[side, d, 1] = imag
-
-        def send(i, c):
-            far, near = node_out(d, i)
-
-            @pl.when(d >= 3)
+        for i in range(d + 1):
+            node_copy(d, i).start()
+
+    def node_finish(d):
+        for i in range(d + 1):
+            copy = node_copy(d, i)
+            if d >= 3:
+                copy.wait_send()
+            else:
+                copy.wait()
+
+    def nodes(action):
+        for d in range(1, 5):
+            @pl.when(jnp.logical_and(first <= d, d < last))
             def _():
-                far.start()
-
-            @pl.when(d < 3)
-            def _():
-                near.start()
-
-            return c
-
-        lax.fori_loop(0, d + 1, send, 0)
-        return carry
-
-    def node_finish(d, carry):
-        def finish(i, c):
-            far, near = node_out(d, i)
-
-            @pl.when(d >= 3)
-            def _():
-                far.wait_send()
-
-            @pl.when(d < 3)
-            def _():
-                near.wait()
-
-            return c
-
-        lax.fori_loop(0, d + 1, finish, 0)
-        return carry
+                action(d)
 
     def pick(x):
         out = x[:, 0:64]
@@ -387,12 +352,15 @@
         put(lh, ll, 4 - a, flipped[0:64], flipped[64:128])
 
     y_first(4)
+    y_first(5)
+    y_first(6)
+    y_forward(4)
     piece_wait(0)
     piece_wait(1)
     y_first(0)
     piece_wait(2)
     y_first(1)
-    y_first(5)
+    y_forward(5)
     y_forward(0)
     y_forward(1)
     piece_wait(4)
@@ -401,52 +369,48 @@
     x_first(1)
     piece_wait(3)
     y_first(2)
-    y_first(6)
-    y_forward(4)
-    y_forward(5)
-    x_forward(0)
-    y_forward(3)
-    x_done(0)
-    x_forward(1)
-    y_first(7)
-    y_first(8)
-    y_forward(2)
+    y_forward(6)
     d_root.wait()
     root_out = pltpu.make_async_copy(dl.at[1], out.at[0], os.at[0])
     root_out.start()
     u[...] = jnp.zeros_like(u)
+    y_done(4)
+    leaf_block(0)
+    x_forward(0)
+    y_done(5)
+    leaf_block(1)
+    y_forward(3)
+    x_done(0)
+    y_forward(2)
+    x_forward(1)
+    y_first(7)
+    y_first(8)
     y_done(3)
     core_copy(9).start()
-    y_forward(6)
-    y_done(4)
-    leaf_block(0)
-    y_done(5)
-    leaf_block(1)
+    y_done(6)
+    leaf_block(2)
     core_copy(9).wait_recv()
     prepare(4)
     y_done(2)
     core_copy(8).start()
-    x_done(1)
     forward(4, u, uh, ul)
     y_forward(7)
     core_copy(8).wait_recv()
     prepare(3)
+    forward(3, u, uh, ul)
     core_done(0)
     put(dnh, dnl, 0, d_block(0, 0), d_block(0, 1))
     prepare(1)
     y_forward(8)
-    forward(3, u, uh, ul)
+    x_done(1)
     core_done(1)
     prepare(2)
-    y_done(6)
-    leaf_block(2)
     forward(2, u, uh, ul)
-    lax.fori_loop(first, last, node, 0)
+    nodes(node)
     y_done(7)
     leaf_block(3)
     forward(1, u, uh, ul)
-    for e in range(1, 5):
-        scale(e, u, uh, ul)
+    for e in range(1, 5): scale(e, u, uh, ul)
     y_done(8)
     leaf_block(4)
     put(uh, ul, 0, u[0, 0], u[0, 1])
@@ -478,7 +442,7 @@
             x_copy(c, q).wait_send()
     for q in range(10):
         core_copy(q).wait_send()
-    lax.fori_loop(first, last, node_finish, 0)
+    nodes(node_finish)
     for d in (3, 4):
         @pl.when(is_home(d))
         def _():

time: 92.1 us -> 79 us (0.86); the launches traced: 91.8 us -> 77.6 us
  Pallas kernels: 89.8 us -> 75.4 us
    pallas_call x1, Pallas kernels: 87 us -> 72.5 us  [inverse_blocks(): pl.pallas_call(kernel, out_shape=jax.ShapeDtypeStruct((21, 2, 64, W), F32...]
where the time goes in v3:
time: 79 us; the launch traced here: 77.6 us
  Pallas kernels  75.4 us (95%)
  local copies, waits for them, and re-layouts  1.36 us (2%)
  between operations  0.82 us (1%)
    pallas_call x1, Pallas kernels, inverse_blocks(): pl.pallas_call(kernel, out_shape=jax.ShapeDtypeStruct((21, 2, 64, W), F32...  72.5 us
    pallas_call x1, Pallas kernels, spread_out(): pl.pallas_call(spread, out_shape=(jax.ShapeDtypeStruct((6, 5, 2, 64, W),...  2.88 us

profile of v3, /device:TPU:5, one launch (start us, length us, event | category | flops | bytes accessed | tf_op | source)
XLA Modules:
  0.0 77.6 jit_solution(15928722096306543890)
XLA Ops:
  0.6 1.4 %copy.5.st = s32[1,6,5]{2,1,0:T(8,128)} copy(s32[1,6,5]{1,0,2:T(1,128)} %param.5) | data formatting | bytes 240 | tf_op args[2]
  2.0 72.5 %inverse_blocks.1.src = f32[21,2,64,256]{3,2,1,0:T(8,128)} custom-call(s32[1,6,5]{2,1,0:T(8,128)} %copy.5.st, f32[6,5,2,64,256]{4,3,2,1,0:T(8,128)} %bitcast.4, f32[6,2,64,256]{3,2,1,0:T(8,128)} %bitcast.5), custom_call_target="tpu_custom_call" | custom-call | tf_op jit(solution)/shard_map/inverse_blocks/pallas_call | solution.py:460
  74.5 2.9 %spread_out.1 = (f32[6,5,2,64,256]{4,3,2,1,0:T(8,128)}, f32[6,2,64,256]{3,2,1,0:T(8,128)}) custom-call(f32[21,2,64,256]{3,2,1,0:T(8,128)} %inverse_blocks.1.src), custom_call_target="tpu_custom_call" | custom-call | tf_op jit(solution)/shard_map/spread_out/pallas_call | solution.py:555

commit v4 on v3

--- a/solution.py
+++ b/solution.py
@@ -30,7 +30,7 @@
 
 def kernel(
     st, lp, dg, out,
-    f012, f3, f4, f5, lv, xnh, xnl, xth, xtl, dnh, dnl, u, uh, ul, v, vh, vl, lh, ll, yo, no, dl,
+    f012, f3, f4, f5, lv, xnh, xnl, xth, xtl, dnh, dnl, u, uh, ul, v, vh, vl, lh, ll, yo, no, dl, sv,
     p1r, s0, s1, s2, s3, s4, ys, yr, xs, xr, cs, cr, os, ls, ns, nr,
 ):
     row = lax.axis_index("row")
@@ -65,15 +65,21 @@
         loads.append(pltpu.make_async_copy(lp.at[d, 0:d], lv.at[AT[d] : AT[d] + d], ls.at[d]))
     d_leaf = pltpu.make_async_copy(dg.at[5], dl.at[0], ls.at[0])
     d_root = pltpu.make_async_copy(dg.at[0], dl.at[1], ls.at[6])
-    for copy in loads + [d_leaf, d_root]:
+    flags = pltpu.make_async_copy(st, sv, ls.at[7])
+    for copy in [flags] + loads + [d_leaf, d_root]:
         copy.start()
+    flags.wait()
+
+    def flag(d, a):
+        return sv[0, d : d + 1, a : a + 1].astype(F32)
+
     loads[0].wait()
     for a in range(5):
-        f5[a, :, row] = f5[a, :, row] * st[0, 5, a].astype(F32)
+        f5[a, :, row] = f5[a, :, row] * flag(5, a)
     for d in range(1, 5):
         loads[d].wait()
         for a in range(d):
-            lv[AT[d] + a] = lv[AT[d] + a] * st[0, d, a].astype(F32)
+            lv[AT[d] + a] = lv[AT[d] + a] * flag(d, a)
 
     callers = 5
     for d in range(5):
@@ -460,7 +466,7 @@
     return pl.pallas_call(
         kernel,
         out_shape=jax.ShapeDtypeStruct((21, 2, 64, W), F32),
-        in_specs=[pl.BlockSpec(memory_space=pltpu.SMEM), any_spec, any_spec],
+        in_specs=[any_spec, any_spec, any_spec],
         out_specs=any_spec,
         scratch_shapes=[
             vmem((6, 2, 4, 4, 2, 8, W), F32),
@@ -478,6 +484,7 @@
             vmem((6, 2, 64, W), F32),
             vmem((2, 5, 2, 64, W), F32),
             vmem((2, 2, 64, W), F32),
+            vmem((1, 6, 5), jnp.int32),
             dma((5, 2)),
             dma((31, 1)),
             dma((15, 2)),
@@ -491,7 +498,7 @@
             dma((10,)),
             dma((10,)),
             dma((3,)),
-            dma((7,)),
+            dma((8,)),
             dma((5, 5)),
             dma((5, 5)),
         ],

time: 79 us -> 78.2 us (0.990)
  Pallas kernels: 75.4 us -> 74.6 us
where the time goes in v4:
time: 78.2 us; the launch traced here: 76.8 us
  Pallas kernels  74.6 us (95%)
  local copies, waits for them, and re-layouts  1.36 us (2%)
  between operations  0.82 us (1%)
    pallas_call x1, Pallas kernels, inverse_blocks(): pl.pallas_call(kernel, out_shape=jax.ShapeDtypeStruct((21, 2, 64, W), F32...  71.7 us
    pallas_call x1, Pallas kernels, spread_out(): pl.pallas_call(spread, out_shape=(jax.ShapeDtypeStruct((6, 5, 2, 64, W),...  2.88 us

profile of v4, /device:TPU:5, one launch (start us, length us, event | category | flops | bytes accessed | tf_op | source)
XLA Modules:
  0.0 76.8 jit_solution(13928503891547564587)
XLA Ops:
  0.6 1.4 %copy.5.st = s32[1,6,5]{2,1,0:T(8,128)} copy(s32[1,6,5]{1,0,2:T(1,128)} %param.5) | data formatting | bytes 240 | tf_op args[2]
  2.0 71.7 %inverse_blocks.1.src = f32[21,2,64,256]{3,2,1,0:T(8,128)} custom-call(s32[1,6,5]{2,1,0:T(8,128)} %copy.5.st, f32[6,5,2,64,256]{4,3,2,1,0:T(8,128)} %bitcast.4, f32[6,2,64,256]{3,2,1,0:T(8,128)} %bitcast.5), custom_call_target="tpu_custom_call" | custom-call | tf_op jit(solution)/shard_map/inverse_blocks/pallas_call | solution.py:466
  73.7 2.9 %spread_out.1 = (f32[6,5,2,64,256]{4,3,2,1,0:T(8,128)}, f32[6,2,64,256]{3,2,1,0:T(8,128)}) custom-call(f32[21,2,64,256]{3,2,1,0:T(8,128)} %inverse_blocks.1.src), custom_call_target="tpu_custom_call" | custom-call | tf_op jit(solution)/shard_map/spread_out/pallas_call | solution.py:562
